TPU v7x, 32 devices: a whole 2x2x4 slice. The times are simulated.
32 devices in a mesh: row: 2 (over core), col: 4 (over y, x), ch: 4 (over z).
Axes of the slice: x: 2, y: 2, z: 4, core: 2. Of those that a mesh axis runs over, the one named last changes fastest.
Arguments:
- grad_out: float32 [4096, 1024], P(('row', 'col'), 'ch'), may hold values from -6 to 6
- relu_mask: int32 [4096, 1024], P(('row', 'col'), 'ch'), may hold values 0 or 1
- saved_agg: float32 [4096, 1024], P(('row', 'col'), 'ch'), may hold values from -0.1875 to 0.1875
- weight: float32 [1024, 1024], P('ch'), may hold values from -0.1875 to 0.1875
- tile_vals: float32 [2, 4, 128, 128, 128], P('row', 'col'), may hold values from -0.125 to 0.125
- tile_pos: int32 [2, 4, 128], P('row', 'col'), may hold values from 0 to 127, as said below
- tile_count: int32 [2, 4], P('row', 'col'), may hold values from 32 to 128, as said below
Outputs:
- weight_grad: float32 [1024, 1024], P(('row', 'col'), 'ch')
- input_grad: float32 [4096, 1024], P('col', 'ch')
Inputs may be any that keep to these rules, and one draw needn't show every extreme that they name: `tile_pos`: each block's entries are a permutation of 0 to 127; the first tile_count of them are the block's nonzero tiles, the others list its zero tiles and their slots' values are ignored. `tile_count`: some block is full in every draw.
All inputs are finite; a program needn't handle non-finite values. No bound on the sum of `relu_mask` on one device may be relied on, other than what follows from the above.
Results may differ from a plain program's by a relative error of at most 0.0003.
Values sent between devices are 32-bit elements; how exact they have to be, the bound alone decides.
A program may use at most 128 MiB of HBM per device.

v0:
```python
import jax
import jax.numpy as jnp
from jax import lax
from jax.sharding import PartitionSpec as P

TILE = 128
OUT_TILES = 16
IN_TILES = 8


HIGHEST = lax.Precision.HIGHEST


def block_grad(tile_set, positions, live_count, grad_rows):
    slot_total = tile_set.shape[0]
    channels = grad_rows.shape[1]
    active = (jnp.arange(slot_total, dtype=jnp.int32) < live_count).astype(jnp.float32)
    out_tile = positions // IN_TILES
    in_tile = positions % IN_TILES
    blocks = grad_rows.reshape(OUT_TILES, TILE, channels)
    picked = jnp.take(blocks, out_tile, axis=0)
    product = jnp.einsum("tij,tif->tjf", tile_set, picked, precision=HIGHEST)
    onehot = (in_tile[:, None] == jnp.arange(IN_TILES, dtype=jnp.int32)[None, :]).astype(
        jnp.float32
    ) * active[:, None]
    summed = jnp.einsum("tc,tjf->cjf", onehot, product, precision=HIGHEST)
    return summed.reshape(IN_TILES * TILE, channels)


def per_device(grad_out, relu_mask, saved_agg, weight, tile_vals, tile_pos, tile_count):
    masked = grad_out * relu_mask.astype(jnp.float32)
    contract_rows = (((0,), (0,)), ((), ()))
    full_masked = lax.all_gather(masked, "ch", axis=1, tiled=True)
    partial_value = lax.dot_general(
        saved_agg, full_masked, contract_rows, precision=HIGHEST, preferred_element_type=jnp.float32
    )
    regrouped = lax.all_to_all(partial_value, "ch", split_axis=1, concat_axis=0, tiled=True)
    weight_grad = lax.psum_scatter(regrouped, ("row", "col"), scatter_dimension=0, tiled=True)
    agg_grad = lax.dot_general(
        full_masked,
        weight,
        (((1,), (1,)), ((), ())),
        precision=HIGHEST,
        preferred_element_type=jnp.float32,
    )
    grad_rows = lax.all_gather(agg_grad, "col", axis=0, tiled=True)
    partial_input = block_grad(tile_vals[0, 0], tile_pos[0, 0], tile_count[0, 0], grad_rows)
    input_grad = lax.psum(partial_input, "row")
    return (weight_grad, input_grad)


def solution(mesh):
    in_specs = (
        P(("row", "col"), "ch"),
        P(("row", "col"), "ch"),
        P(("row", "col"), "ch"),
        P("ch", None),
        P("row", "col", None, None, None),
        P("row", "col", None),
        P("row", "col"),
    )
    out_specs = (P(("row", "col"), "ch"), P("col", "ch"))
    return jax.shard_map(
        per_device, mesh=mesh, in_specs=in_specs, out_specs=out_specs, check_vma=False
    )
```

profile of v0, /device:TPU:4, one launch (start us, length us, event | category | flops | bytes accessed | tf_op | source)
XLA Modules:
  0.0 202.4 jit_solution(18225518108952591362)
XLA Ops:
  7.2 0.0 all-gather.3.cloned.1.call-start
  7.2 2.1 %convert_multiply_fusion = f32[512,256]{1,0:T(8,128)} fusion(f32[512,256]{1,0:T(8,128)} %param.7, s32[512,256]{1,0:T(8,128)} %param.8), kind=kLoop, calls=%fused_computation.8 | loop fusion | flops 262144 | bytes 1572864 | tf_op jit(solution)/shard_map/mul | solution.py:31
  9.4 0.0 all-gather.3.cloned.1.call-update
  9.4 0.0 all-gather.5.cloned.1.call-start
  9.4 47.6 %all-gather.3.cloned.1.call-done = f32[512,1024]{1,0:T(8,128)} async-done(((f32[512,256]{1,0:T(8,128)}), f32[512,1024]{1,0:T(8,128)}) %all-gather.3.cloned.1.call-update) | async-done | bytes 2097168 | tf_op jit(solution)/shard_map/all_gather | solution.py:33
  57.0 4.2 %fusion.16 = f32[512,256]{1,0:T(8,128)} fusion(f32[512,1024]{1,0:T(8,128)} %all-gather.3.cloned.1.call-done, f32[256,1024]{1,0:T(8,128)S(1)} %copy-done), kind=kOutput, calls=%fused_computation.35 | convolution fusion | flops 1610612736 | bytes 3670016 | tf_op jit(solution)/shard_map/dot_general | solution.py:39
  61.3 6.1 %fusion.15 = f32[1024,256]{1,0:T(8,128)} fusion(f32[512,1024]{1,0:T(8,128)} %all-gather.3.cloned.1.call-done, f32[512,256]{1,0:T(8,128)} %param.9), kind=kOutput, calls=%fused_computation.34 | convolution fusion | flops 1610612736 | bytes 3670016 | tf_op jit(solution)/shard_map/dot_general | solution.py:34
  67.4 3.5 %all-to-all-start = ((f32[256,4,256]{0,2,1:T(8,128)}), f32[256,4,256]{0,2,1:T(8,128)S(1)}, u32[]{:S(2)}, u32[]{:S(2)}) async-start(f32[256,4,256]{0,2,1:T(8,128)} %bitcast.1), calls=%async_computation | async-start | bytes 2097152 | tf_op jit(solution)/shard_map/all_to_all | solution.py:37
  70.9 0.0 reduce-scatter.2.cloned.1.call-start
  71.6 0.7 fusion.12
  72.3 0.7 compare_and_fusion
  72.9 0.7 and_select_fusion.2
  73.6 23.1 %all-to-all-done = f32[256,4,256]{0,2,1:T(8,128)S(1)} async-done(((f32[256,4,256]{0,2,1:T(8,128)}), f32[256,4,256]{0,2,1:T(8,128)S(1)}, u32[]{:S(2)}, u32[]{:S(2)}) %all-to-all-start) | async-done | bytes 1048608 | tf_op jit(solution)/shard_map/all_to_all | solution.py:37
  96.7 1.3 copy.10
  98.0 0.2 all-reduce.2.cloned.1.call-start
  98.3 0.0 all-gather.5.cloned.1.call-done
  98.3 11.7 %gather_fusion = f32[128,128,256]{2,1,0:T(8,128)} fusion(f32[16,128,256]{2,1,0:T(8,128)} %bitcast.51, s32[1024]{0:T(1024)S(1)} %pad_clamp_fusion), kind=kCustom, calls=%fused_computation | custom fusion | bytes 33554944 | tf_op jit(solution)/shard_map/jit(_take)/gather | solution.py:21
  110.0 34.6 %fusion.2 = f32[128,256,128]{2,1,0:T(8,128)} fusion(f32[128,128,256]{2,1,0:T(8,128)} %gather_fusion, f32[1,1,128,128,128]{4,3,2,1,0:T(8,128)} %param.11, pred[128]{0:T(512)(128)(4,1)S(1)} %compare_and_fusion), kind=kOutput, calls=%fused_computation.3 | convolution fusion | flops 6446645248 | bytes 41943168 | tf_op jit(solution)/shard_map/tij,tif->tjf/dot_general | solution.py:22
  144.6 17.8 %copy.12 = f32[128,256,128]{1,0,2:T(8,128)} copy(f32[128,256,128]{2,1,0:T(8,128)} %fusion.2) | data formatting | bytes 33554432 | tf_op jit(solution)/shard_map/tij,tif->tjf/dot_general | solution.py:22
  162.3 10.8 %fusion = f32[8,128,256]{2,0,1:T(8,128)S(1)} fusion(f32[128,256,128]{1,0,2:T(8,128)} %copy.12, f32[128]{0:T(128)S(1)} %compare_convert_fusion, s32[128]{0:T(128)S(1)} %and_select_fusion.2), kind=kOutput, calls=%fused_computation.1 | convolution fusion | flops 402655232 | bytes 17826816 | tf_op jit(solution)/shard_map/tc,tjf->cjf/dot_general | solution.py:26
  173.2 1.3 copy.11
  174.5 0.0 reduce-scatter.2.cloned.1.call-done
  174.6 19.0 %all-reduce.2.cloned.1.call-done = f32[1024,256]{1,0:T(8,128)} async-done(((f32[1024,256]{1,0:T(8,128)}), f32[1024,256]{1,0:T(8,128)}) %all-reduce.2.cloned.1.call-update) | async-done | bytes 1048592 | tf_op jit(solution)/shard_map/psum | solution.py:48
  193.6 2.3 %copy.15 = f32[1024,256]{1,0:T(8,128)} copy(f32[1024,256]{1,0:T(8,128)} %all-reduce.2.cloned.1.call-done) | data formatting | bytes 2097152
  (9 shorter events, 0.1 us)
Async XLA Ops:
  7.2 49.9 %copy-start = (f32[256,1024]{1,0:T(8,128)S(1)}, f32[256,1024]{1,0:T(8,128)}, u32[]{:S(2)}) copy-start(f32[256,1024]{1,0:T(8,128)} %param.10) | copy-start | bytes 3145732
  7.2 49.8 %all-gather.3.cloned.1.call-start = ((), (), s32[]{:S(2)}) async-start(), calls=%async_computation.2 | async-start | bytes 2621440 | tf_op jit(solution)/shard_map/all_gather | solution.py:33
  9.4 88.9 %all-gather.5.cloned.1.call-start = ((), (), s32[]{:S(2)}) async-start(), calls=%async_computation.4 | async-start | bytes 2621440 | tf_op jit(solution)/shard_map/all_gather | solution.py:46
  67.4 29.4 %all-to-all-start = ((f32[256,4,256]{0,2,1:T(8,128)}), f32[256,4,256]{0,2,1:T(8,128)S(1)}, u32[]{:S(2)}, u32[]{:S(2)}) async-start(f32[256,4,256]{0,2,1:T(8,128)} %bitcast.1), calls=%async_computation | async-start | bytes 2097152 | tf_op jit(solution)/shard_map/all_to_all | solution.py:37
  70.9 103.7 %reduce-scatter.2.cloned.1.call-start = ((), (), s32[]{:S(2)}) async-start(), calls=%async_computation.3 | async-start | bytes 1179648 | tf_op jit(solution)/shard_map/reduce_scatter | solution.py:38
  98.0 95.5 %all-reduce.2.cloned.1.call-start = ((), (), s32[]{:S(2)}) async-start(), calls=%async_computation.5 | async-start | bytes 2097152 | tf_op jit(solution)/shard_map/psum | solution.py:48
  144.6 51.3 %copy-start.1 = (f32[256,1024]{1,0:T(8,128)S(1)}, f32[256,1024]{1,0:T(8,128)}, u32[]{:S(2)}) copy-start(f32[256,1024]{1,0:T(8,128)} %param.10) | copy-start | bytes 3145732
Sparse Core Ops, SparseCore 0:
  10.1 46.8 all-gather.2
  61.4 33.9 all-gather.4
  99.2 35.9 reduce-scatter.1
  174.6 18.8 all-reduce.1
where the time goes:
time: 204 us; the launch traced here: 202 us
  waiting for transfers between devices  89.8 us (44%)
  matrix products  55.7 us (27%)
  local copies, waits for them, and re-layouts  34.4 us (17%)
  between operations  14.5 us (7%)
  other arithmetic  4.15 us (2%)
  starting transfers between devices  3.86 us (2%)
    all_gather x1, waiting for transfers between devices, per_device(): full_masked = lax.all_gather(masked, 'ch', axis=1, tiled=True)  47.6 us
    dot_general x1, matrix products, block_grad(): product = jnp.einsum('tij,tif->tjf', tile_set, picked, precision=HIGHEST)  34.6 us
    all_to_all x1, waiting for transfers between devices, per_device(): lax.all_to_all(partial_value, 'ch', split_axis=1, concat_axis=0, tiled=True)  23.1 us
    psum x1, waiting for transfers between devices, per_device(): input_grad = lax.psum(partial_input, 'row')  19 us
    dot_general x1, local copies, waits for them, and re-layouts, block_grad(): product = jnp.einsum('tij,tif->tjf', tile_set, picked, precision=HIGHEST)  17.8 us
    gather x1, local copies, waits for them, and re-layouts, block_grad(): picked = jnp.take(blocks, out_tile, axis=0)  11.7 us
    dot_general x1, matrix products, block_grad(): summed = jnp.einsum('tc,tjf->cjf', onehot, product, precision=HIGHEST)  10.8 us
    dot_general x1, matrix products, per_device(): lax.dot_general(saved_agg, full_masked, contract_rows, precision=HIGHEST,...  6.08 us
  transfers between devices with their start and end apart: 5, of which 3 were waited for; matrix products, arithmetic and copies ran while one was open for 42% of the time, Pallas kernels for 0%

commit v1 on v0

v1 whole, which is shorter than its diff:
```python
import functools

import jax
import jax.numpy as jnp
from jax import lax
from jax.experimental import pallas as pl
from jax.experimental.pallas import tpu as pltpu
from jax.sharding import PartitionSpec as P

TILE = 128
MESH = pl.DeviceIdType.MESH
F32 = jnp.float32
BF16 = jnp.bfloat16


def split(x):
    hi = x.astype(BF16)
    return hi, (x - hi.astype(F32)).astype(BF16)


def nn(a, b):
    return lax.dot_general(a, b, (((1,), (0,)), ((), ())), preferred_element_type=F32)


def nt(a, b):
    return lax.dot_general(a, b, (((1,), (1,)), ((), ())), preferred_element_type=F32)


def kernel(
    R, C, N, K,
    slot_ref, g_ref, mask_ref, sa_hbm, w_hbm, tiles_hbm,
    wg_ref, ig_ref,
    M, G, tiles, at_hi, at_lo, w_f, w_hi, w_lo, sa, g_hi, g_lo, acc,
    wgp, wgr, wgs, wgc, wgo, igr,
    local_sem, zsend, zrecv, csend, crecv, wrsend, wrrecv, wcsend, wcrecv, wfsend, wfrecv,
    irsend, irrecv, iasend, iarecv,
):
    r, c, z = lax.axis_index("row"), lax.axis_index("col"), lax.axis_index("ch")
    HB, D = M.shape[2], M.shape[3]
    RC = R * C
    per = RC // N
    blk = wgp.shape[1]
    slots = tiles.shape[0]
    IN = acc.shape[0]
    in_tiles = IN // TILE
    tpb = HB // TILE
    piece = IN // R

    cp_w = pltpu.make_async_copy(w_hbm, w_f, local_sem.at[0])
    cp_sa = pltpu.make_async_copy(sa_hbm, sa, local_sem.at[1])
    cp_t = pltpu.make_async_copy(tiles_hbm, tiles, local_sem.at[2])
    cp_w.start()
    cp_sa.start()
    cp_t.start()

    def dev(r_, c_, z_):
        return {"row": r_, "col": c_, "ch": z_}

    q = r * C + c
    d_idx = z * per + q // N
    d_r, d_c, d_z = d_idx // C, d_idx % C, q % N
    s_q = (q % per) * N + z
    s_r, s_c, s_z = s_q // C, s_q % C, q // per
    away = jnp.logical_not((d_r == r) & (d_c == c) & (d_z == z))

    barrier = pltpu.get_barrier_semaphore()

    def hello(r_, c_, z_):
        pl.semaphore_signal(barrier, inc=1, device_id=dev(r_, c_, z_), device_id_type=MESH)

    for j in range(1, R):
        hello((r + j) % R, c, z)
    for j in range(1, C):
        hello(r, (c + j) % C, z)

    @pl.when(z > 0)
    def _():
        hello(r, c, z - 1)

    @pl.when(z < N - 1)
    def _():
        hello(r, c, z + 1)

    @pl.when(away)
    def _():
        hello(d_r, d_c, d_z)
        hello(s_r, s_c, s_z)

    def own(k):
        rows = pl.ds(pl.multiple_of(k * HB, HB), HB)
        M[z, k] = g_ref[rows, :] * mask_ref[rows, :].astype(F32)

    own(0)
    own(1)
    one_if = lambda cond: jnp.where(cond, 1, 0)
    greeted = R - 1 + C - 1 + one_if(z > 0) + one_if(z < N - 1) + 2 * one_if(away)
    pl.semaphore_wait(barrier, greeted)

    def zcopy(origin, k, step):
        way = 0 if step < 0 else 1
        return pltpu.make_async_remote_copy(
            src_ref=M.at[origin, k], dst_ref=M.at[origin, k],
            send_sem=zsend.at[way, origin, k], recv_sem=zrecv.at[origin, k],
            device_id=dev(r, c, z + step), device_id_type=MESH,
        )

    def own_send(k):
        @pl.when(z > 0)
        def _():
            zcopy(z, k, -1).start()

        @pl.when(z < N - 1)
        def _():
            zcopy(z, k, 1).start()

    own_send(0)
    own_send(1)
    acc[...] = jnp.zeros_like(acc)
    wgp[...] = jnp.zeros_like(wgp)
    cp_w.wait()
    for n in range(N):
        cols = slice(n * D, (n + 1) * D)
        w_hi[:, cols], w_lo[:, cols] = split(w_f[:, cols])
    cp_sa.wait()
    cp_t.wait()

    def prep(k, cc):
        for t in range(tpb):
            def one(i, _):
                p = ((cc * K + k) * tpb + t) * in_tiles + i
                v = slot_ref[p]
                tile = tiles[lax.rem(v, slots)]
                tile = jnp.where(v < slots, tile, jnp.zeros_like(tile))
                hi, lo = split(tile.T)
                rows = pl.ds(pl.multiple_of(i * TILE, TILE), TILE)
                cols = slice(cc * HB + t * TILE, cc * HB + (t + 1) * TILE)
                at_hi[k, rows, cols] = hi
                at_lo[k, rows, cols] = lo
                return 0

            lax.fori_loop(0, in_tiles, one, 0, unroll=2)

    def ccopy(k, j):
        return pltpu.make_async_remote_copy(
            src_ref=G.at[k, c], dst_ref=G.at[k, c],
            send_sem=csend.at[k, j], recv_sem=crecv.at[k, j],
            device_id=dev(r, (c + j) % C, z), device_id_type=MESH,
        )

    def cwait(k, j):
        o = (c + C - j) % C
        return pltpu.make_async_remote_copy(
            src_ref=G.at[k, o], dst_ref=G.at[k, o],
            send_sem=csend.at[k, j], recv_sem=crecv.at[k, j],
            device_id=dev(r, (c + j) % C, z), device_id_type=MESH,
        )

    def consume(k):
        for j in range(1, C):
            cwait(k, j).wait_recv()
        for n in range(C):
            rows = slice(n * HB, (n + 1) * HB)
            g_hi[rows, :], g_lo[rows, :] = split(G[k, n])

        def part(i, _):
            rows = pl.ds(pl.multiple_of(i * 256, 256), 256)
            a = at_hi[k, rows, :]
            acc[rows, :] += nn(a, g_hi[...]) + nn(a, g_lo[...]) + nn(at_lo[k, rows, :], g_hi[...])
            return 0

        lax.fori_loop(0, IN // 256, part, 0)

    groups = [[] for _ in range(N - 1)]
    for cc in range(C):
        groups[cc * (N - 1) // C].append(cc)

    def body(k, _):
        for d in range(1, N):
            for cc in groups[d - 1]:
                prep(k, cc)

            @pl.when(z >= d)
            def _():
                zcopy(z - d, k, 1).wait_recv()

                @pl.when(z < N - 1)
                def _():
                    zcopy(z - d, k, 1).start()

            @pl.when(z + d < N)
            def _():
                zcopy(z + d, k, -1).wait_recv()

                @pl.when(z > 0)
                def _():
                    zcopy(z + d, k, -1).start()

            if d == 1:
                @pl.when(k + 2 < K)
                def _():
                    own(k + 2)
                    own_send(k + 2)

        agg = jnp.zeros((HB, D), F32)
        for n in range(N):
            cols = slice(n * D, (n + 1) * D)
            hi, lo = split(M[n, k])
            agg += nt(hi, w_hi[:, cols]) + nt(lo, w_hi[:, cols]) + nt(hi, w_lo[:, cols])
        G[k, c] = agg
        for j in range(1, C):
            ccopy(k, j).start()

        rows = pl.ds(pl.multiple_of(k * HB, HB), HB)
        s_hi, s_lo = split(sa[rows, :].T)
        for n in range(N):
            hi, lo = split(M[n, k])
            res = nn(s_hi, hi) + nn(s_hi, lo) + nn(s_lo, hi)
            for h in range(per):
                wgp[h * N + n] += res[h * blk:(h + 1) * blk, :]

        @pl.when(k > 0)
        def _():
            consume(k - 1)

        return 0

    lax.fori_loop(0, K, body, 0)

    def wrcopy(j):
        t = (r + j) % R
        return pltpu.make_async_remote_copy(
            src_ref=wgp.at[pl.ds(t * C, C)], dst_ref=wgr.at[j],
            send_sem=wrsend.at[j], recv_sem=wrrecv.at[j],
            device_id=dev(t, c, z), device_id_type=MESH,
        )

    def wccopy(j):
        t = (c + j) % C
        return pltpu.make_async_remote_copy(
            src_ref=wgs.at[t], dst_ref=wgc.at[j],
            send_sem=wcsend.at[j], recv_sem=wcrecv.at[j],
            device_id=dev(r, t, z), device_id_type=MESH,
        )

    wfcopy = pltpu.make_async_remote_copy(
        src_ref=wgo, dst_ref=wg_ref, send_sem=wfsend, recv_sem=wfrecv,
        device_id=dev(d_r, d_c, d_z), device_id_type=MESH,
    )

    def ircopy(j):
        t = (r + j) % R
        return pltpu.make_async_remote_copy(
            src_ref=acc.at[pl.ds(pl.multiple_of(t * piece, piece), piece)], dst_ref=igr.at[j],
            send_sem=irsend.at[j], recv_sem=irrecv.at[j],
            device_id=dev(t, c, z), device_id_type=MESH,
        )

    mine = pl.ds(pl.multiple_of(r * piece, piece), piece)

    def iacopy(j):
        return pltpu.make_async_remote_copy(
            src_ref=ig_ref.at[mine], dst_ref=ig_ref.at[mine],
            send_sem=iasend.at[j], recv_sem=iarecv.at[j],
            device_id=dev((r + j) % R, c, z), device_id_type=MESH,
        )

    def iawait(j):
        theirs = pl.ds(pl.multiple_of(((r + R - j) % R) * piece, piece), piece)
        return pltpu.make_async_remote_copy(
            src_ref=ig_ref.at[theirs], dst_ref=ig_ref.at[theirs],
            send_sem=iasend.at[j], recv_sem=iarecv.at[j],
            device_id=dev((r + j) % R, c, z), device_id_type=MESH,
        )

    for j in range(1, R):
        wrcopy(j).start()
    for j in range(1, R):
        wrcopy(j).wait_recv()
    total = wgp[pl.ds(r * C, C)]
    for j in range(1, R):
        total += wgr[j]
    wgs[...] = total
    for j in range(1, C):
        wccopy(j).start()

    consume(K - 1)
    for j in range(1, R):
        ircopy(j).start()
    for j in range(1, R):
        ircopy(j).wait_recv()
    summed = acc[mine, :]
    for j in range(1, R):
        summed += igr[j]
    ig_ref[mine, :] = summed
    for j in range(1, R):
        iacopy(j).start()

    for j in range(1, C):
        wccopy(j).wait_recv()
    wpart = wgs[c]
    for j in range(1, C):
        wpart += wgc[j]

    @pl.when(away)
    def _():
        wgo[...] = wpart
        wfcopy.start()
        wfcopy.wait()

    @pl.when(jnp.logical_not(away))
    def _():
        wg_ref[...] = wpart

    for j in range(1, R):
        iawait(j).wait_recv()

    for j in range(1, R):
        wrcopy(j).wait_send()
        ircopy(j).wait_send()
        iacopy(j).wait_send()
    for j in range(1, C):
        wccopy(j).wait_send()

    def drain(k, _):
        for j in range(1, C):
            ccopy(k, j).wait_send()
        for n in range(N):
            @pl.when((z > 0) & (z <= n))
            def _():
                zcopy(n, k, -1).wait_send()

            @pl.when((z < N - 1) & (z >= n))
            def _():
                zcopy(n, k, 1).wait_send()

        return 0

    lax.fori_loop(0, K, drain, 0)


def per_device(R, C, N, grad_out, relu_mask, saved_agg, weight, tile_vals, tile_pos, tile_count):
    H, D = grad_out.shape
    F = weight.shape[1]
    tiles = tile_vals[0, 0]
    slots = tiles.shape[0]
    out_rows = C * H
    IN = slots * TILE * TILE // out_rows
    HB = TILE
    K = H // HB
    blk = F // (R * C)
    s = jnp.arange(slots, dtype=jnp.int32)
    code = jnp.where(s < tile_count[0, 0], s, s + slots)
    where = jnp.sum(jnp.where(tile_pos[0, 0][None, :] == s[:, None], code[None, :], 0), axis=1).astype(jnp.int32)
    vmem = pl.BlockSpec(memory_space=pltpu.VMEM)
    hbm = pl.BlockSpec(memory_space=pl.ANY)
    dma = pltpu.SemaphoreType.DMA
    return pl.pallas_call(
        functools.partial(kernel, R, C, N, K),
        out_shape=(
            jax.ShapeDtypeStruct((blk, D), F32),
            jax.ShapeDtypeStruct((IN, D), F32),
        ),
        in_specs=[pl.BlockSpec(memory_space=pltpu.SMEM), vmem, vmem, hbm, hbm, hbm],
        out_specs=(vmem, vmem),
        scratch_shapes=[
            pltpu.VMEM((N, K, HB, D), F32),
            pltpu.VMEM((K, C, HB, D), F32),
            pltpu.VMEM((slots, TILE, TILE), F32),
            pltpu.VMEM((K, IN, C * HB), BF16),
            pltpu.VMEM((K, IN, C * HB), BF16),
            pltpu.VMEM((D, F), F32),
            pltpu.VMEM((D, F), BF16),
            pltpu.VMEM((D, F), BF16),
            pltpu.VMEM((H, D), F32),
            pltpu.VMEM((C * HB, D), BF16),
            pltpu.VMEM((C * HB, D), BF16),
            pltpu.VMEM((IN, D), F32),
            pltpu.VMEM((R * C, blk, D), F32),
            pltpu.VMEM((R, C, blk, D), F32),
            pltpu.VMEM((C, blk, D), F32),
            pltpu.VMEM((C, blk, D), F32),
            pltpu.VMEM((blk, D), F32),
            pltpu.VMEM((R, IN // R, D), F32),
            dma((3,)),
            dma((2, N, K)), dma((N, K)),
            dma((K, C)), dma((K, C)),
            dma((R,)), dma((R,)),
            dma((C,)), dma((C,)),
            dma, dma,
            dma((R,)), dma((R,)),
            dma((R,)), dma((R,)),
        ],
        compiler_params=pltpu.CompilerParams(
            collective_id=0, has_side_effects=True, vmem_limit_bytes=60 * 1024 * 1024
        ),
    )(where, grad_out, relu_mask, saved_agg, weight, tiles)


def solution(mesh):
    in_specs = (
        P(("row", "col"), "ch"),
        P(("row", "col"), "ch"),
        P(("row", "col"), "ch"),
        P("ch", None),
        P("row", "col", None, None, None),
        P("row", "col", None),
        P("row", "col"),
    )
    out_specs = (P(("row", "col"), "ch"), P("col", "ch"))
    R, C, N = mesh.shape["row"], mesh.shape["col"], mesh.shape["ch"]
    return jax.shard_map(
        functools.partial(per_device, R, C, N), mesh=mesh, in_specs=in_specs, out_specs=out_specs, check_vma=False
    )
```

time: 204 us -> 73.6 us (0.36)
  waiting for transfers between devices: 89.8 us -> 0 us
  Pallas kernels: 0 us -> 67 us
  matrix products: 55.7 us -> 0 us
  local copies, waits for them, and re-layouts: 34.4 us -> 3.83 us
  between operations: 14.5 us -> 1.29 us
  starting transfers between devices: 3.86 us -> 0 us
  other arithmetic: 4.15 us -> 1.29 us
    pallas_call x0 -> x1, Pallas kernels: none -> 67 us  [per_device(): pl.pallas_call(functools.partial(kernel, R, C, N, K), out_shape=(jax.Shap...]
    dot_general x4 -> x0, matrix products: 55.7 us -> none  [the longest x1 34.6 us: block_grad(): product = jnp.einsum('tij,tif->tjf', tile_set, picked, precision=HIGHEST)]
    all_gather x2 -> x0, waiting for transfers between devices: 47.6 us -> none  [the longest x1 47.6 us: per_device(): full_masked = lax.all_gather(masked, 'ch', axis=1, tiled=True)]
    all_to_all x1 -> x0, waiting for transfers between devices: 23.1 us -> none  [per_device(): lax.all_to_all(partial_value, 'ch', split_axis=1, concat_axis=0, tiled=True)]
    dot_general x2 -> x0, local copies, waits for them, and re-layouts: 19.1 us -> none  [the longest x1 17.8 us: block_grad(): product = jnp.einsum('tij,tif->tjf', tile_set, picked, precision=HIGHEST)]
    psum x1 -> x0, waiting for transfers between devices: 19 us -> none  [per_device(): input_grad = lax.psum(partial_input, 'row')]
    gather x1 -> x0, local copies, waits for them, and re-layouts: 11.7 us -> none  [block_grad(): picked = jnp.take(blocks, out_tile, axis=0)]
    all_to_all x1 -> x0, starting transfers between devices: 3.52 us -> none  [per_device(): lax.all_to_all(partial_value, 'ch', split_axis=1, concat_axis=0, tiled=True)]
  transfers between devices with their start and end apart: 5 -> 0, of which waited for: 3 -> 0; matrix products, arithmetic and copies ran while one was open for 42% -> 0% of each run, Pallas kernels for 0% -> 0%
where the time goes in v1:
time: 73.6 us; the launch traced here: 73.4 us
  Pallas kernels  67 us (91%)
  local copies, waits for them, and re-layouts  3.83 us (5%)
  other arithmetic  1.29 us (2%)
  between operations  1.29 us (2%)
    pallas_call x1, Pallas kernels, per_device(): pl.pallas_call(functools.partial(kernel, R, C, N, K), out_shape=(jax.Shap...  67 us
    unnamed x2, local copies, waits for them, and re-layouts  3.83 us

profile of v1, /device:TPU:4, one launch (start us, length us, event | category | flops | bytes accessed | tf_op | source)
XLA Modules:
  0.0 73.4 jit_solution(7293174123966625398)
XLA Ops:
  1.3 1.3 %select_reduce_fusion.slot_ref = s32[128]{0:T(128)} fusion(s32[128]{0:T(128)S(1)} %compare_select_fusion, s32[128]{0:T(128)} %bitcast.5), kind=kLoop, calls=%fused_computation | loop fusion | flops 49024 | bytes 1536 | tf_op jit(solution)/shard_map/reduce_sum | solution.py:353
  2.6 67.0 %shard_map.86 = (f32[128,256]{1,0:T(8,128)}, f32[1024,256]{1,0:T(8,128)}) custom-call(s32[128]{0:T(128)} %select_reduce_fusion.slot_ref, f32[512,256]{1,0:T(8,128)} %g_ref.1, s32[512,256]{1,0:T(8,128)} %mask_ref.1, f32[512,256]{1,0:T(8,128)} %sa_hbm.1, f32[256,1024]{1,0:T(8,128)} %w_hbm.1, f32[128,128,128]{2,1,0:T(8,128)} %bitcast.4), custom_call_target="tpu_custom_call" | custom-call | tf_op jit(solution)/shard_map/pallas_call | solution.py:357
  69.6 1.6 %copy.12 = f32[128,256]{1,0:T(8,128)} copy(f32[128,256]{1,0:T(8,128)} %get-tuple-element.4) | data formatting | bytes 262144
  71.1 2.3 %copy.13 = f32[1024,256]{1,0:T(8,128)} copy(f32[1024,256]{1,0:T(8,128)} %get-tuple-element.5) | data formatting | bytes 2097152
  (1 shorter events, 0.0 us)

commit v2 on v1

--- a/solution.py
+++ b/solution.py
@@ -29,18 +29,19 @@
 def kernel(
     R, C, N, K,
     slot_ref, g_ref, mask_ref, sa_hbm, w_hbm, tiles_hbm,
-    wg_ref, ig_ref,
-    M, G, tiles, at_hi, at_lo, w_f, w_hi, w_lo, sa, g_hi, g_lo, acc,
-    wgp, wgr, wgs, wgc, wgo, igr,
+    wg_ref, ig_ref, igr,
+    M, G, tiles, at_hi, at_lo, w_f, w_hi, w_lo, sa, sa_far, g_hi, g_lo,
+    wgp, wgr, wgs, wgc, wgo,
     local_sem, zsend, zrecv, csend, crecv, wrsend, wrrecv, wcsend, wcrecv, wfsend, wfrecv,
-    irsend, irrecv, iasend, iarecv,
+    irsend, irrecv, iasend, iarecv, sasend, sarecv,
 ):
     r, c, z = lax.axis_index("row"), lax.axis_index("col"), lax.axis_index("ch")
     HB, D = M.shape[2], M.shape[3]
     RC = R * C
     per = RC // N
-    blk = wgp.shape[1]
+    blk = wgp.shape[2]
     slots = tiles.shape[0]
+    acc = ig_ref
     IN = acc.shape[0]
     in_tiles = IN // TILE
     tpb = HB // TILE
@@ -57,11 +58,26 @@
         return {"row": r_, "col": c_, "ch": z_}
 
     q = r * C + c
-    d_idx = z * per + q // N
-    d_r, d_c, d_z = d_idx // C, d_idx % C, q % N
+    mid = (z > 0) & (z < N - 1)
+    hosts = (z == 1) | (z == N - 2)
+    far = jnp.where(z == 1, 0, N - 1)
+    step_in = jnp.where(z == 0, 1, -1)
+
+    def dest(zi):
+        idx = zi * per + q // N
+        return idx // C, idx % C, q % N
+
+    def is_me(o):
+        return (o[0] == r) & (o[1] == c) & (o[2] == z)
+
+    dests = (dest(z), dest(far))
+    active = (mid, hosts)
+    away = tuple(a & jnp.logical_not(is_me(o)) for a, o in zip(active, dests))
+    home = tuple(a & is_me(o) for a, o in zip(active, dests))
     s_q = (q % per) * N + z
-    s_r, s_c, s_z = s_q // C, s_q % C, q // per
-    away = jnp.logical_not((d_r == r) & (d_c == c) & (d_z == z))
+    s_z = jnp.minimum(jnp.maximum(q // per, 1), N - 2)
+    source = (s_q // C, s_q % C, s_z)
+    fed = jnp.logical_not(is_me(source))
 
     barrier = pltpu.get_barrier_semaphore()
 
@@ -81,10 +97,14 @@
     def _():
         hello(r, c, z + 1)
 
-    @pl.when(away)
+    for s in range(2):
+        @pl.when(away[s])
+        def _():
+            hello(*dests[s])
+
+    @pl.when(fed)
     def _():
-        hello(d_r, d_c, d_z)
-        hello(s_r, s_c, s_z)
+        hello(*source)
 
     def own(k):
         rows = pl.ds(pl.multiple_of(k * HB, HB), HB)
@@ -93,7 +113,7 @@
     own(0)
     own(1)
     one_if = lambda cond: jnp.where(cond, 1, 0)
-    greeted = R - 1 + C - 1 + one_if(z > 0) + one_if(z < N - 1) + 2 * one_if(away)
+    greeted = R - 1 + C - 1 + one_if(z > 0) + one_if(z < N - 1) + one_if(fed) + one_if(away[0]) + one_if(away[1])
     pl.semaphore_wait(barrier, greeted)
 
     def zcopy(origin, k, step):
@@ -104,6 +124,14 @@
             device_id=dev(r, c, z + step), device_id_type=MESH,
         )
 
+    def sacopy(k, step):
+        rows = pl.ds(pl.multiple_of(k * HB, HB), HB)
+        return pltpu.make_async_remote_copy(
+            src_ref=sa.at[rows], dst_ref=sa_far.at[rows],
+            send_sem=sasend.at[k], recv_sem=sarecv.at[k],
+            device_id=dev(r, c, z + step), device_id_type=MESH,
+        )
+
     def own_send(k):
         @pl.when(z > 0)
         def _():
@@ -113,6 +141,11 @@
         def _():
             zcopy(z, k, 1).start()
 
+        @pl.when(jnp.logical_not(mid))
+        def _():
+            sacopy(k, step_in).start()
+
+    cp_sa.wait()
     own_send(0)
     own_send(1)
     acc[...] = jnp.zeros_like(acc)
@@ -121,7 +154,6 @@
     for n in range(N):
         cols = slice(n * D, (n + 1) * D)
         w_hi[:, cols], w_lo[:, cols] = split(w_f[:, cols])
-    cp_sa.wait()
     cp_t.wait()
 
     def prep(k, cc):
@@ -170,6 +202,28 @@
 
         lax.fori_loop(0, IN // 256, part, 0)
 
+    def wrcopy(s, j):
+        t = (r + j) % R
+        return pltpu.make_async_remote_copy(
+            src_ref=wgp.at[s, pl.ds(t * C, C)], dst_ref=wgr.at[s, j],
+            send_sem=wrsend.at[s, j], recv_sem=wrrecv.at[s, j],
+            device_id=dev(t, c, z), device_id_type=MESH,
+        )
+
+    def wccopy(s, j):
+        t = (c + j) % C
+        return pltpu.make_async_remote_copy(
+            src_ref=wgs.at[s, t], dst_ref=wgc.at[s, j],
+            send_sem=wcsend.at[s, j], recv_sem=wcrecv.at[s, j],
+            device_id=dev(r, t, z), device_id_type=MESH,
+        )
+
+    def wfcopy(s):
+        return pltpu.make_async_remote_copy(
+            src_ref=wgo.at[s], dst_ref=wg_ref, send_sem=wfsend.at[s], recv_sem=wfrecv,
+            device_id=dev(*dests[s]), device_id_type=MESH,
+        )
+
     groups = [[] for _ in range(N - 1)]
     for cc in range(C):
         groups[cc * (N - 1) // C].append(cc)
@@ -211,12 +265,31 @@
             ccopy(k, j).start()
 
         rows = pl.ds(pl.multiple_of(k * HB, HB), HB)
-        s_hi, s_lo = split(sa[rows, :].T)
-        for n in range(N):
-            hi, lo = split(M[n, k])
-            res = nn(s_hi, hi) + nn(s_hi, lo) + nn(s_lo, hi)
-            for h in range(per):
-                wgp[h * N + n] += res[h * blk:(h + 1) * blk, :]
+
+        def grad(s, ref):
+            s_hi, s_lo = split(ref[rows, :].T)
+            for n in range(N):
+                hi, lo = split(M[n, k])
+                res = nn(s_hi, hi) + nn(s_hi, lo) + nn(s_lo, hi)
+                for h in range(per):
+                    wgp[s, h * N + n] += res[h * blk:(h + 1) * blk, :]
+
+        @pl.when(mid)
+        def _():
+            grad(0, sa)
+
+        @pl.when(hosts)
+        def _():
+            sacopy(k, step_in).wait_recv()
+            grad(1, sa_far)
+
+        @pl.when(k == K - 1)
+        def _():
+            for s in range(2):
+                @pl.when(active[s])
+                def _():
+                    for j in range(1, R):
+                        wrcopy(s, j).start()
 
         @pl.when(k > 0)
         def _():
@@ -225,32 +298,13 @@
         return 0
 
     lax.fori_loop(0, K, body, 0)
-
-    def wrcopy(j):
-        t = (r + j) % R
-        return pltpu.make_async_remote_copy(
-            src_ref=wgp.at[pl.ds(t * C, C)], dst_ref=wgr.at[j],
-            send_sem=wrsend.at[j], recv_sem=wrrecv.at[j],
-            device_id=dev(t, c, z), device_id_type=MESH,
-        )
-
-    def wccopy(j):
-        t = (c + j) % C
-        return pltpu.make_async_remote_copy(
-            src_ref=wgs.at[t], dst_ref=wgc.at[j],
-            send_sem=wcsend.at[j], recv_sem=wcrecv.at[j],
-            device_id=dev(r, t, z), device_id_type=MESH,
-        )
-
-    wfcopy = pltpu.make_async_remote_copy(
-        src_ref=wgo, dst_ref=wg_ref, send_sem=wfsend, recv_sem=wfrecv,
-        device_id=dev(d_r, d_c, d_z), device_id_type=MESH,
-    )
 
     def ircopy(j):
         t = (r + j) % R
-        return pltpu.make_async_remote_copy(
-            src_ref=acc.at[pl.ds(pl.multiple_of(t * piece, piece), piece)], dst_ref=igr.at[j],
+        whole = R == 2
+        rows = pl.ds(0, IN) if whole else pl.ds(pl.multiple_of(t * piece, piece), piece)
+        return pltpu.make_async_remote_copy(
+            src_ref=acc.at[rows], dst_ref=igr if whole else igr.at[j],
             send_sem=irsend.at[j], recv_sem=irrecv.at[j],
             device_id=dev(t, c, z), device_id_type=MESH,
         )
@@ -272,56 +326,77 @@
             device_id=dev((r + j) % R, c, z), device_id_type=MESH,
         )
 
-    for j in range(1, R):
-        wrcopy(j).start()
-    for j in range(1, R):
-        wrcopy(j).wait_recv()
-    total = wgp[pl.ds(r * C, C)]
-    for j in range(1, R):
-        total += wgr[j]
-    wgs[...] = total
-    for j in range(1, C):
-        wccopy(j).start()
-
+    def fold_rows(s):
+        for j in range(1, R):
+            wrcopy(s, j).wait_recv()
+        total = wgp[s, pl.ds(r * C, C)]
+        for j in range(1, R):
+            total += wgr[s, j]
+        wgs[s] = total
+        for j in range(1, C):
+            wccopy(s, j).start()
+
+    def fold_cols(s):
+        for j in range(1, C):
+            wccopy(s, j).wait_recv()
+        total = wgs[s, c]
+        for j in range(1, C):
+            total += wgc[s, j]
+
+        @pl.when(away[s])
+        def _():
+            wgo[s] = total
+            wfcopy(s).start()
+
+        @pl.when(home[s])
+        def _():
+            wg_ref[...] = total
+
+    for s in range(2):
+        pl.when(active[s])(functools.partial(fold_rows, s))
     consume(K - 1)
     for j in range(1, R):
         ircopy(j).start()
+    for s in range(2):
+        pl.when(active[s])(functools.partial(fold_cols, s))
     for j in range(1, R):
         ircopy(j).wait_recv()
-    summed = acc[mine, :]
+    if R > 2:
+        summed = acc[mine, :]
+        for j in range(1, R):
+            summed += igr[j]
+        ig_ref[mine, :] = summed
+        for j in range(1, R):
+            iacopy(j).start()
+        for j in range(1, R):
+            iawait(j).wait_recv()
+
+    @pl.when(fed)
+    def _():
+        wfcopy(0).wait_recv()
+
+    for s in range(2):
+        @pl.when(active[s])
+        def _():
+            for j in range(1, R):
+                wrcopy(s, j).wait_send()
+            for j in range(1, C):
+                wccopy(s, j).wait_send()
+
+        @pl.when(away[s])
+        def _():
+            wfcopy(s).wait_send()
+
     for j in range(1, R):
-        summed += igr[j]
-    ig_ref[mine, :] = summed
-    for j in range(1, R):
-        iacopy(j).start()
-
-    for j in range(1, C):
-        wccopy(j).wait_recv()
-    wpart = wgs[c]
-    for j in range(1, C):
-        wpart += wgc[j]
-
-    @pl.when(away)
-    def _():
-        wgo[...] = wpart
-        wfcopy.start()
-        wfcopy.wait()
-
-    @pl.when(jnp.logical_not(away))
-    def _():
-        wg_ref[...] = wpart
-
-    for j in range(1, R):
-        iawait(j).wait_recv()
-
-    for j in range(1, R):
-        wrcopy(j).wait_send()
         ircopy(j).wait_send()
-        iacopy(j).wait_send()
-    for j in range(1, C):
-        wccopy(j).wait_send()
+        if R > 2:
+            iacopy(j).wait_send()
 
     def drain(k, _):
+        @pl.when(jnp.logical_not(mid))
+        def _():
+            sacopy(k, step_in).wait_send()
+
         for j in range(1, C):
             ccopy(k, j).wait_send()
         for n in range(N):
@@ -354,14 +429,17 @@
     vmem = pl.BlockSpec(memory_space=pltpu.VMEM)
     hbm = pl.BlockSpec(memory_space=pl.ANY)
     dma = pltpu.SemaphoreType.DMA
-    return pl.pallas_call(
+    assert N >= 4
+    igr_shape = (IN, D) if R == 2 else (R, IN // R, D)
+    wg, ig, igr = pl.pallas_call(
         functools.partial(kernel, R, C, N, K),
         out_shape=(
             jax.ShapeDtypeStruct((blk, D), F32),
             jax.ShapeDtypeStruct((IN, D), F32),
+            jax.ShapeDtypeStruct(igr_shape, F32),
         ),
         in_specs=[pl.BlockSpec(memory_space=pltpu.SMEM), vmem, vmem, hbm, hbm, hbm],
-        out_specs=(vmem, vmem),
+        out_specs=(vmem, vmem, vmem),
         scratch_shapes=[
             pltpu.VMEM((N, K, HB, D), F32),
             pltpu.VMEM((K, C, HB, D), F32),
@@ -372,28 +450,39 @@
             pltpu.VMEM((D, F), BF16),
             pltpu.VMEM((D, F), BF16),
             pltpu.VMEM((H, D), F32),
+            pltpu.VMEM((H, D), F32),
             pltpu.VMEM((C * HB, D), BF16),
             pltpu.VMEM((C * HB, D), BF16),
-            pltpu.VMEM((IN, D), F32),
-            pltpu.VMEM((R * C, blk, D), F32),
-            pltpu.VMEM((R, C, blk, D), F32),
-            pltpu.VMEM((C, blk, D), F32),
-            pltpu.VMEM((C, blk, D), F32),
-            pltpu.VMEM((blk, D), F32),
-            pltpu.VMEM((R, IN // R, D), F32),
+            pltpu.VMEM((2, R * C, blk, D), F32),
+            pltpu.VMEM((2, R, C, blk, D), F32),
+            pltpu.VMEM((2, C, blk, D), F32),
+            pltpu.VMEM((2, C, blk, D), F32),
+            pltpu.VMEM((2, blk, D), F32),
             dma((3,)),
             dma((2, N, K)), dma((N, K)),
             dma((K, C)), dma((K, C)),
-            dma((R,)), dma((R,)),
-            dma((C,)), dma((C,)),
-            dma, dma,
+            dma((2, R)), dma((2, R)),
+            dma((2, C)), dma((2, C)),
+            dma((2,)), dma,
             dma((R,)), dma((R,)),
             dma((R,)), dma((R,)),
+            dma((K,)), dma((K,)),
         ],
         compiler_params=pltpu.CompilerParams(
             collective_id=0, has_side_effects=True, vmem_limit_bytes=60 * 1024 * 1024
         ),
     )(where, grad_out, relu_mask, saved_agg, weight, tiles)
+
+    def finish(wg_in, a, b, wg_out, ig_out):
+        wg_out[...] = wg_in[...]
+        ig_out[...] = a[...] + b[...] if R == 2 else a[...]
+
+    return pl.pallas_call(
+        finish,
+        out_shape=(jax.ShapeDtypeStruct((blk, D), F32), jax.ShapeDtypeStruct((IN, D), F32)),
+        in_specs=[vmem, vmem, vmem if R == 2 else hbm],
+        out_specs=(vmem, vmem),
+    )(wg, ig, igr)
 
 
 def solution(mesh):

time: 73.6 us -> 75.7 us (1.029)
  the two profiles are of different devices: /device:TPU:4 before, /device:TPU:0 now
where the time goes in v2:
time: 75.7 us; the launch traced here: 75.5 us
  Pallas kernels  72.9 us (96%)
  other arithmetic  1.29 us (2%)
  between operations  1.29 us (2%)
    pallas_call x1, Pallas kernels, per_device(): pl.pallas_call(functools.partial(kernel, R, C, N, K), out_shape=(jax.Shap...  70.2 us
    pallas_call x1, Pallas kernels, per_device(): pl.pallas_call(finish, out_shape=(jax.ShapeDtypeStruct((blk, D), F32), ja...  2.67 us

profile of v2, /device:TPU:0, one launch (start us, length us, event | category | flops | bytes accessed | tf_op | source)
XLA Modules:
  0.0 75.5 jit_solution(12336309578699530270)
XLA Ops:
  1.3 1.3 %select_reduce_fusion.slot_ref = s32[128]{0:T(128)} fusion(s32[128]{0:T(128)S(1)} %compare_select_fusion, s32[128]{0:T(128)} %bitcast.5), kind=kLoop, calls=%fused_computation | loop fusion | flops 49024 | bytes 1536 | tf_op jit(solution)/shard_map/reduce_sum | solution.py:428
  2.6 70.2 %shard_map.86 = (f32[128,256]{1,0:T(8,128)}, f32[1024,256]{1,0:T(8,128)}, f32[1024,256]{1,0:T(8,128)}) custom-call(s32[128]{0:T(128)} %select_reduce_fusion.slot_ref, f32[512,256]{1,0:T(8,128)} %g_ref.1, s32[512,256]{1,0:T(8,128)} %mask_ref.1, f32[512,256]{1,0:T(8,128)} %sa_hbm.1, f32[256,1024]{1,0:T(8,128)} %w_hbm.1, f32[128,128,128]{2,1,0:T(8,128)} %bitcast.4), custom_call_target="tpu_custom_call" | custom-call | tf_op jit(solution)/shard_map/pallas_call | solution.py:434
  72.8 2.7 %shard_map.87 = (f32[128,256]{1,0:T(8,128)}, f32[1024,256]{1,0:T(8,128)}) custom-call(f32[128,256]{1,0:T(8,128)} %get-tuple-element.5.wg_in, f32[1024,256]{1,0:T(8,128)} %get-tuple-element.6.a, f32[1024,256]{1,0:T(8,128)} %get-tuple-element.7.b), custom_call_target="tpu_custom_call" | custom-call | tf_op jit(solution)/shard_map/pallas_call | solution.py:480
  (1 shorter events, 0.0 us)

commit v3 on v1

--- a/solution.py
+++ b/solution.py
@@ -29,9 +29,9 @@
 def kernel(
     R, C, N, K,
     slot_ref, g_ref, mask_ref, sa_hbm, w_hbm, tiles_hbm,
-    wg_ref, ig_ref,
-    M, G, tiles, at_hi, at_lo, w_f, w_hi, w_lo, sa, g_hi, g_lo, acc,
-    wgp, wgr, wgs, wgc, wgo, igr,
+    wg_ref, ig_ref, igr,
+    M, G, tiles, at_hi, at_lo, w_f, w_hi, w_lo, sa, g_hi, g_lo,
+    wgp, wgr, wgs, wgc, wgo,
     local_sem, zsend, zrecv, csend, crecv, wrsend, wrrecv, wcsend, wcrecv, wfsend, wfrecv,
     irsend, irrecv, iasend, iarecv,
 ):
@@ -41,6 +41,7 @@
     per = RC // N
     blk = wgp.shape[1]
     slots = tiles.shape[0]
+    acc = ig_ref
     IN = acc.shape[0]
     in_tiles = IN // TILE
     tpb = HB // TILE
@@ -170,15 +171,20 @@
 
         lax.fori_loop(0, IN // 256, part, 0)
 
+    def wrcopy(j):
+        t = (r + j) % R
+        return pltpu.make_async_remote_copy(
+            src_ref=wgp.at[pl.ds(t * C, C)], dst_ref=wgr.at[j],
+            send_sem=wrsend.at[j], recv_sem=wrrecv.at[j],
+            device_id=dev(t, c, z), device_id_type=MESH,
+        )
+
     groups = [[] for _ in range(N - 1)]
     for cc in range(C):
-        groups[cc * (N - 1) // C].append(cc)
+        groups[cc * max(N - 2, 1) // C].append(cc)
 
     def body(k, _):
         for d in range(1, N):
-            for cc in groups[d - 1]:
-                prep(k, cc)
-
             @pl.when(z >= d)
             def _():
                 zcopy(z - d, k, 1).wait_recv()
@@ -200,6 +206,9 @@
                 def _():
                     own(k + 2)
                     own_send(k + 2)
+
+            for cc in groups[d - 1]:
+                prep(k, cc)
 
         agg = jnp.zeros((HB, D), F32)
         for n in range(N):
@@ -218,6 +227,11 @@
             for h in range(per):
                 wgp[h * N + n] += res[h * blk:(h + 1) * blk, :]
 
+        @pl.when(k == K - 1)
+        def _():
+            for j in range(1, R):
+                wrcopy(j).start()
+
         @pl.when(k > 0)
         def _():
             consume(k - 1)
@@ -225,14 +239,6 @@
         return 0
 
     lax.fori_loop(0, K, body, 0)
-
-    def wrcopy(j):
-        t = (r + j) % R
-        return pltpu.make_async_remote_copy(
-            src_ref=wgp.at[pl.ds(t * C, C)], dst_ref=wgr.at[j],
-            send_sem=wrsend.at[j], recv_sem=wrrecv.at[j],
-            device_id=dev(t, c, z), device_id_type=MESH,
-        )
 
     def wccopy(j):
         t = (c + j) % C
@@ -249,8 +255,10 @@
 
     def ircopy(j):
         t = (r + j) % R
-        return pltpu.make_async_remote_copy(
-            src_ref=acc.at[pl.ds(pl.multiple_of(t * piece, piece), piece)], dst_ref=igr.at[j],
+        whole = R == 2
+        rows = pl.ds(0, IN) if whole else pl.ds(pl.multiple_of(t * piece, piece), piece)
+        return pltpu.make_async_remote_copy(
+            src_ref=acc.at[rows], dst_ref=igr if whole else igr.at[j],
             send_sem=irsend.at[j], recv_sem=irrecv.at[j],
             device_id=dev(t, c, z), device_id_type=MESH,
         )
@@ -272,8 +280,6 @@
             device_id=dev((r + j) % R, c, z), device_id_type=MESH,
         )
 
-    for j in range(1, R):
-        wrcopy(j).start()
     for j in range(1, R):
         wrcopy(j).wait_recv()
     total = wgp[pl.ds(r * C, C)]
@@ -286,15 +292,6 @@
     consume(K - 1)
     for j in range(1, R):
         ircopy(j).start()
-    for j in range(1, R):
-        ircopy(j).wait_recv()
-    summed = acc[mine, :]
-    for j in range(1, R):
-        summed += igr[j]
-    ig_ref[mine, :] = summed
-    for j in range(1, R):
-        iacopy(j).start()
-
     for j in range(1, C):
         wccopy(j).wait_recv()
     wpart = wgs[c]
@@ -312,12 +309,22 @@
         wg_ref[...] = wpart
 
     for j in range(1, R):
-        iawait(j).wait_recv()
+        ircopy(j).wait_recv()
+    if R > 2:
+        summed = acc[mine, :]
+        for j in range(1, R):
+            summed += igr[j]
+        ig_ref[mine, :] = summed
+        for j in range(1, R):
+            iacopy(j).start()
+        for j in range(1, R):
+            iawait(j).wait_recv()
 
     for j in range(1, R):
         wrcopy(j).wait_send()
         ircopy(j).wait_send()
-        iacopy(j).wait_send()
+        if R > 2:
+            iacopy(j).wait_send()
     for j in range(1, C):
         wccopy(j).wait_send()
 
@@ -354,14 +361,16 @@
     vmem = pl.BlockSpec(memory_space=pltpu.VMEM)
     hbm = pl.BlockSpec(memory_space=pl.ANY)
     dma = pltpu.SemaphoreType.DMA
-    return pl.pallas_call(
+    igr_shape = (IN, D) if R == 2 else (R, IN // R, D)
+    wg, ig, igr = pl.pallas_call(
         functools.partial(kernel, R, C, N, K),
         out_shape=(
             jax.ShapeDtypeStruct((blk, D), F32),
             jax.ShapeDtypeStruct((IN, D), F32),
+            jax.ShapeDtypeStruct(igr_shape, F32),
         ),
         in_specs=[pl.BlockSpec(memory_space=pltpu.SMEM), vmem, vmem, hbm, hbm, hbm],
-        out_specs=(vmem, vmem),
+        out_specs=(vmem, vmem, vmem),
         scratch_shapes=[
             pltpu.VMEM((N, K, HB, D), F32),
             pltpu.VMEM((K, C, HB, D), F32),
@@ -374,13 +383,11 @@
             pltpu.VMEM((H, D), F32),
             pltpu.VMEM((C * HB, D), BF16),
             pltpu.VMEM((C * HB, D), BF16),
-            pltpu.VMEM((IN, D), F32),
             pltpu.VMEM((R * C, blk, D), F32),
             pltpu.VMEM((R, C, blk, D), F32),
             pltpu.VMEM((C, blk, D), F32),
             pltpu.VMEM((C, blk, D), F32),
             pltpu.VMEM((blk, D), F32),
-            pltpu.VMEM((R, IN // R, D), F32),
             dma((3,)),
             dma((2, N, K)), dma((N, K)),
             dma((K, C)), dma((K, C)),
@@ -394,6 +401,17 @@
             collective_id=0, has_side_effects=True, vmem_limit_bytes=60 * 1024 * 1024
         ),
     )(where, grad_out, relu_mask, saved_agg, weight, tiles)
+
+    def finish(wg_in, a, b, wg_out, ig_out):
+        wg_out[...] = wg_in[...]
+        ig_out[...] = a[...] + b[...] if R == 2 else a[...]
+
+    return pl.pallas_call(
+        finish,
+        out_shape=(jax.ShapeDtypeStruct((blk, D), F32), jax.ShapeDtypeStruct((IN, D), F32)),
+        in_specs=[vmem, vmem, vmem if R == 2 else hbm],
+        out_specs=(vmem, vmem),
+    )(wg, ig, igr)
 
 
 def solution(mesh):

time: 73.6 us -> 71.6 us (0.973)
  local copies, waits for them, and re-layouts: 3.83 us -> 0 us
  Pallas kernels: 67 us -> 68.8 us
    unnamed x2 -> x0, local copies, waits for them, and re-layouts: 3.83 us -> none
    pallas_call x0 -> x1, Pallas kernels: none -> 2.67 us  [per_device(): pl.pallas_call(finish, out_shape=(jax.ShapeDtypeStruct((blk, D), F32), ja...]
    pallas_call x1, Pallas kernels: 67 us -> 66.2 us  [per_device(): pl.pallas_call(functools.partial(kernel, R, C, N, K), out_shape=(jax.Shap...]
where the time goes in v3:
time: 71.6 us; the launch traced here: 71.4 us
  Pallas kernels  68.8 us (96%)
  other arithmetic  1.29 us (2%)
  between operations  1.29 us (2%)
    pallas_call x1, Pallas kernels, per_device(): pl.pallas_call(functools.partial(kernel, R, C, N, K), out_shape=(jax.Shap...  66.2 us
    pallas_call x1, Pallas kernels, per_device(): pl.pallas_call(finish, out_shape=(jax.ShapeDtypeStruct((blk, D), F32), ja...  2.67 us

profile of v3, /device:TPU:4, one launch (start us, length us, event | category | flops | bytes accessed | tf_op | source)
XLA Modules:
  0.0 71.4 jit_solution(16667991718322448853)
XLA Ops:
  1.3 1.3 %select_reduce_fusion.slot_ref = s32[128]{0:T(128)} fusion(s32[128]{0:T(128)S(1)} %compare_select_fusion, s32[128]{0:T(128)} %bitcast.5), kind=kLoop, calls=%fused_computation | loop fusion | flops 49024 | bytes 1536 | tf_op jit(solution)/shard_map/reduce_sum | solution.py:360
  2.6 66.2 %shard_map.86 = (f32[128,256]{1,0:T(8,128)}, f32[1024,256]{1,0:T(8,128)}, f32[1024,256]{1,0:T(8,128)}) custom-call(s32[128]{0:T(128)} %select_reduce_fusion.slot_ref, f32[512,256]{1,0:T(8,128)} %g_ref.1, s32[512,256]{1,0:T(8,128)} %mask_ref.1, f32[512,256]{1,0:T(8,128)} %sa_hbm.1, f32[256,1024]{1,0:T(8,128)} %w_hbm.1, f32[128,128,128]{2,1,0:T(8,128)} %bitcast.4), custom_call_target="tpu_custom_call" | custom-call | tf_op jit(solution)/shard_map/pallas_call | solution.py:365
  68.7 2.7 %shard_map.87 = (f32[128,256]{1,0:T(8,128)}, f32[1024,256]{1,0:T(8,128)}) custom-call(f32[128,256]{1,0:T(8,128)} %get-tuple-element.5.wg_in, f32[1024,256]{1,0:T(8,128)} %get-tuple-element.6.a, f32[1024,256]{1,0:T(8,128)} %get-tuple-element.7.b), custom_call_target="tpu_custom_call" | custom-call | tf_op jit(solution)/shard_map/pallas_call | solution.py:409
  (1 shorter events, 0.0 us)
